TPU v7x, 32 devices: a whole 2x2x4 slice. The times are simulated.
32 devices in a mesh: lon: 8 (over z, y), lat: 4 (over x, core).
Axes of the slice: x: 2, y: 2, z: 4, core: 2. Of those that a mesh axis runs over, the one named last changes fastest.
Arguments:
- right_side: float32 [1024, 4096], P('lat', 'lon'), may hold values from -6 to 6
- depth_level: int32 [1024, 4096], P('lat', 'lon'), may hold values from 1 to 50
- ocean_mask: int32 [1024, 4096], P('lat', 'lon'), may hold values 0 or 1
Outputs:
- pressure: float32 [1024, 4096], P('lat', 'lon')
- residual: float32 [1024, 4096], P('lat', 'lon')
All inputs are finite; a program needn't handle non-finite values. No bound on the sum of `ocean_mask` on one device may be relied on, other than what follows from the above.
Results may differ from a plain program's by a relative error of at most 0.0003.
Values sent between devices are 32-bit elements; how exact they have to be, the bound alone decides.
A program may use at most 128 MiB of HBM per device.

v0:
```python
import jax
import jax.numpy as jnp
from jax import lax
from jax.sharding import PartitionSpec as P

LEVELS = 4
SWEEPS = 2
COARSE_SWEEPS = 9
DEPTH_LEVELS = 50


OMEGA = 0.8
SIGMA = 1e-05


def with_halo(cells, sides, width, closed):
    for axis, dim in sides:
        count = lax.axis_size(axis)
        ends = count if closed else count - 1
        head = lax.slice_in_dim(cells, 0, width, axis=dim)
        tail = lax.slice_in_dim(cells, cells.shape[dim] - width, cells.shape[dim], axis=dim)
        cells = jnp.concatenate(
            [
                lax.ppermute(tail, axis, [(i, (i + 1) % count) for i in range(ends)]),
                cells,
                lax.ppermute(head, axis, [((i + 1) % count, i) for i in range(ends)]),
            ],
            axis=dim,
        )
    return cells


def local_neighbours(field):
    lon_padded = with_halo(field, (("lon", 1),), 1, True)
    lat_padded = with_halo(field, (("lat", 0),), 1, False)
    return (lon_padded[:, 2:], lon_padded[:, :-2], lat_padded[2:], lat_padded[:-2])


def coefficients(height, scale, finder):
    east_side, west_side, north_side, south_side = finder(height)
    coef_east = jnp.minimum(height, east_side) * scale
    coef_west = jnp.minimum(height, west_side) * scale
    coef_north = jnp.minimum(height, north_side) * scale
    coef_south = jnp.minimum(height, south_side) * scale
    faces = coef_east + coef_west + coef_north + coef_south
    diagonal = SIGMA + faces
    return (coef_east, coef_west, coef_north, coef_south, diagonal, faces)


def keep_active(source, coefs):
    return jnp.where(coefs[5] > 0.0, source, jnp.zeros_like(source))


def operate(field, coefs, finder):
    east_side, west_side, north_side, south_side = finder(field)
    return (
        coefs[4] * field
        - coefs[0] * east_side
        - coefs[1] * west_side
        - coefs[2] * north_side
        - coefs[3] * south_side
    )


def jacobi(field, source, coefs, finder):
    return field + OMEGA * (source - operate(field, coefs, finder)) / coefs[4]


def smooth_zero(source, coefs, finder):
    field = OMEGA * source / coefs[4]
    field = jacobi(field, source, coefs, finder)
    return field


def restrict(field):
    row_count, col_count = field.shape
    return field.reshape(row_count // 2, 2, col_count // 2, 2).mean(axis=(1, 3))


def prolong(field):
    row_count, col_count = field.shape
    return jnp.broadcast_to(field[:, None, :, None], (row_count, 2, col_count, 2)).reshape(
        row_count * 2, col_count * 2
    )


def deep_pad(stacked):
    widened = with_halo(stacked, (("lon", 2),), 2, True)
    return with_halo(widened, (("lat", 1),), 2, False)


def trimmed(padded, margin):
    cut = 2 - margin
    return padded[:, cut : padded.shape[1] - cut, cut : padded.shape[2] - cut]


def margin_sweep(field, margin, known):
    inner = trimmed(known, margin - 1)
    source = inner[0]
    diagonal = inner[1]
    safe_diagonal = jnp.where(diagonal > 0.0, diagonal, jnp.ones_like(diagonal))
    center = field[1:-1, 1:-1]
    applied = (
        diagonal * center
        - inner[2] * field[1:-1, 2:]
        - inner[3] * field[1:-1, :-2]
        - inner[4] * field[2:, 1:-1]
        - inner[5] * field[:-2, 1:-1]
    )
    return center + OMEGA * (source - applied) / safe_diagonal


def local(right_side, depth_level, ocean_mask):
    ocean = ocean_mask.astype(jnp.float32)
    height = ocean * depth_level.astype(jnp.float32) / DEPTH_LEVELS
    source = right_side
    saved = []
    for level in range(LEVELS - 1):
        coefs = coefficients(height, 0.25**level, local_neighbours)
        source = keep_active(source, coefs)
        iterate = smooth_zero(source, coefs, local_neighbours)
        saved.append((iterate, source, coefs))
        source = restrict(source - operate(iterate, coefs, local_neighbours))
        height = restrict(height)
    coefs = coefficients(height, 0.25 ** (LEVELS - 1), local_neighbours)
    source = keep_active(source, coefs)
    known = deep_pad(jnp.stack([source, coefs[4], coefs[0], coefs[1], coefs[2], coefs[3]]))
    iterate = OMEGA * source / coefs[4]
    for pair in range((COARSE_SWEEPS - 1) // 2):
        padded = deep_pad(iterate[None])[0]
        padded = margin_sweep(padded, 2, known)
        iterate = margin_sweep(padded, 1, known)
    for level in reversed(range(LEVELS - 1)):
        previous, source, coefs = saved[level]
        iterate = previous + prolong(iterate)
        for sweep in range(SWEEPS):
            iterate = jacobi(iterate, source, coefs, local_neighbours)
    source, coefs = (saved[0][1], saved[0][2])
    return (iterate, source - operate(iterate, coefs, local_neighbours))


def solution(mesh):
    placed = (P("lat", "lon"), P("lat", "lon"), P("lat", "lon"))
    return jax.shard_map(
        local,
        mesh=mesh,
        in_specs=placed,
        out_specs=(P("lat", "lon"), P("lat", "lon")),
        check_vma=False,
    )
```

profile of v0, /device:TPU:0, one launch (start us, length us, event | category | flops | bytes accessed | tf_op | source)
XLA Modules:
  0.0 472.3 jit_solution(4294676721657418797)
XLA Ops:
  8.1 3.1 collective-permute-start
  11.2 34.8 %reshape.36 = f32[128,2,256,2]{3,2,1,0:T(8,128)} reshape(f32[256,512]{1,0:T(8,128)S(1)} %multiply_multiply_fusion) | data formatting | bytes 1048576 | tf_op jit(solution)/shard_map/reshape | solution.py:77
  46.1 13.2 %reduce_sum.54 = f32[128,256]{1,0:T(8,128)S(1)} reduce(f32[128,2,256,2]{3,2,1,0:T(8,128)} %reshape.36, f32[]{:T(128)} %constant.9.clone.1), dimensions={1,3}, to_apply=%region_0.1 | reduce | flops 98304 | bytes 655364 | tf_op jit(solution)/shard_map/reduce_sum | solution.py:77
  59.4 4.0 collective-permute-start.11
  63.5 9.8 %div.99 = f32[64,2,128,2]{3,2,1,0:T(8,128)} reshape(f32[128,256]{1,0:T(8,128)S(1)} %broadcast_multiply_fusion) | data formatting | bytes 262144 | tf_op jit(solution)/shard_map/div | solution.py:77
  73.3 4.5 reduce_sum.56
  79.7 4.7 collective-permute-start.7
  86.5 3.6 collective-permute-done.4
  90.0 4.8 %collective-permute-done.5 = f32[256,1]{1,0:T(8,128)S(1)} collective-permute-done((f32[256,1]{1,0:T(8,128)S(1)}, f32[256,1]{1,0:T(8,128)S(1)}, u32[]{:S(2)}, u32[]{:S(2)}) %collective-permute-start.5) | collective-permute-done | bytes 1056 | tf_op jit(solution)/shard_map/ppermute | solution.py:24
  97.1 3.0 collective-permute-start.15
  102.8 3.2 collective-permute-done.12
  107.2 3.2 collective-permute-done.13
  110.4 4.7 collective-permute-start.8
  117.9 34.9 %reshape.37 = f32[128,2,256,2]{3,2,1,0:T(8,128)} reshape(f32[256,512]{1,0:T(8,128)S(1)} %fusion.35) | data formatting | bytes 1048576 | tf_op jit(solution)/shard_map/reshape | solution.py:77
  152.8 13.3 %reduce_sum.55 = f32[128,256]{1,0:T(8,128)S(1)} reduce(f32[128,2,256,2]{3,2,1,0:T(8,128)} %reshape.37, f32[]{:T(128)} %constant.9.clone.1), dimensions={1,3}, to_apply=%region_1.2 | reduce | flops 98304 | bytes 655364 | tf_op jit(solution)/shard_map/reduce_sum | solution.py:77
  183.3 3.0 collective-permute-start.27
  192.1 3.9 collective-permute-done.25
  199.2 9.8 %reshape.38 = f32[64,2,128,2]{3,2,1,0:T(8,128)} reshape(f32[128,256]{1,0:T(8,128)S(1)} %fusion.85) | data formatting | bytes 262144 | tf_op jit(solution)/shard_map/reshape | solution.py:77
  209.0 4.5 reduce_sum.57
  215.7 3.0 collective-permute-start.31
  218.7 4.0 collective-permute-start.28
  224.7 4.7 collective-permute-done.29
  231.5 3.4 collective-permute-start.39
  238.9 3.2 collective-permute-start.35
  243.1 4.7 collective-permute-start.32
  254.0 4.7 collective-permute-start.41
  263.4 4.7 collective-permute-start.45
  271.0 5.4 %collective-permute-start.46 = (f32[6,2,68]{2,1,0:T(2,128)S(1)}, f32[6,2,68]{2,1,0:T(2,128)S(1)}, u32[]{:S(2)}, u32[]{:S(2)}) collective-permute-start(f32[6,2,68]{2,1,0:T(2,128)S(1)} %get-tuple-element.29), channel_id=1, source_target_pairs={{0,1},{1,2},{2,3},{4,5},{5,6},{6,7},{8,9},{9,10},{10,11},{12,13},{... | collective-permute-start | bytes 9800 | tf_op jit(solution)/shard_map/ppermute | solution.py:24
  281.9 4.7 collective-permute-start.49
  288.4 3.1 collective-permute-start.50
  296.4 4.8 %collective-permute-start.53 = (f32[1,32,2]{2,1,0:T(8,128)S(1)}, f32[1,32,2]{2,1,0:T(8,128)S(1)}, u32[]{:S(2)}, u32[]{:S(2)}) collective-permute-start(f32[1,32,2]{2,1,0:T(8,128)S(1)} %get-tuple-element.84), channel_id=1, source_target_pairs={{4,0},{8,4},{12,8},{16,12},{20,16},{24,20},{28,24},{0,28},{5,1},{9... | collective-permute-start | bytes 776 | tf_op jit(solution)/shard_map/ppermute | solution.py:26
  302.9 3.4 collective-permute-start.54
  311.0 4.8 %collective-permute-start.57 = (f32[1,32,2]{2,1,0:T(8,128)S(1)}, f32[1,32,2]{2,1,0:T(8,128)S(1)}, u32[]{:S(2)}, u32[]{:S(2)}) collective-permute-start(f32[1,32,2]{2,1,0:T(8,128)S(1)} %get-tuple-element.82), channel_id=1, source_target_pairs={{4,0},{8,4},{12,8},{16,12},{20,16},{24,20},{28,24},{0,28},{5,1},{9... | collective-permute-start | bytes 776 | tf_op jit(solution)/shard_map/ppermute | solution.py:26
  317.5 3.4 collective-permute-start.58
  329.8 4.9 %collective-permute-start.63 = (f32[1,128]{1,0:T(1,128)S(1)}, f32[1,128]{1,0:T(1,128)S(1)}, u32[]{:S(2)}, u32[]{:S(2)}) collective-permute-start(f32[1,128]{1,0:T(1,128)S(1)} %get-tuple-element.68), channel_id=1, source_target_pairs={{0,1},{1,2},{2,3},{4,5},{5,6},{6,7},{8,9},{9,10},{10,11},{12,13},{... | collective-permute-start | bytes 1544 | tf_op jit(solution)/shard_map/ppermute | solution.py:24
  334.6 4.8 %collective-permute-start.60 = (f32[64,1]{1,0:T(8,128)S(1)}, f32[64,1]{1,0:T(8,128)S(1)}, u32[]{:S(2)}, u32[]{:S(2)}) collective-permute-start(f32[64,1]{1,0:T(8,128)S(1)} %get-tuple-element.65), channel_id=1, source_target_pairs={{4,0},{8,4},{12,8},{16,12},{20,16},{24,20},{28,24},{0,28},{5,1},{9... | collective-permute-start | bytes 776 | tf_op jit(solution)/shard_map/ppermute | solution.py:26
  341.1 5.0 %collective-permute-done.61 = f32[64,1]{1,0:T(8,128)S(1)} collective-permute-done((f32[64,1]{1,0:T(8,128)S(1)}, f32[64,1]{1,0:T(8,128)S(1)}, u32[]{:S(2)}, u32[]{:S(2)}) %collective-permute-start.61) | collective-permute-done | bytes 288 | tf_op jit(solution)/shard_map/ppermute | solution.py:24
  348.5 3.0 collective-permute-start.67
  359.3 4.0 broadcast_in_dim.35
  363.3 6.9 %reshape.41 = f32[128,256]{1,0:T(8,128)S(1)} reshape(f32[64,2,128,2]{3,2,1,0:T(8,128)} %broadcast_in_dim.35) | data formatting | bytes 262144 | tf_op jit(solution)/shard_map/reshape | solution.py:82
  383.5 3.0 collective-permute-start.75
  394.0 11.4 %broadcast_in_dim.36 = f32[128,2,256,2]{3,2,1,0:T(8,128)} broadcast(f32[128,256]{1,0:T(8,128)S(1)} %fusion.64), dimensions={0,2} | broadcast | bytes 655360 | tf_op jit(solution)/shard_map/broadcast_in_dim | solution.py:82
  405.4 24.2 %reshape.42 = f32[256,512]{1,0:T(8,128)S(1)} reshape(f32[128,2,256,2]{3,2,1,0:T(8,128)} %broadcast_in_dim.36) | data formatting | bytes 1048576 | tf_op jit(solution)/shard_map/reshape | solution.py:82
  431.0 3.0 collective-permute-start.79
  436.3 3.6 collective-permute-done.76
  439.8 3.1 collective-permute-done.77
  450.2 3.6 collective-permute-done.80
  464.5 3.6 collective-permute-done.84
  (289 shorter events, 158.0 us)
Async XLA Ops:
  1.9 75.9 %collective-permute-start.3 = (f32[1,512]{1,0:T(1,128)S(1)}, f32[1,512]{1,0:T(1,128)S(1)}, u32[]{:S(2)}, u32[]{:S(2)}) collective-permute-start(f32[1,512]{1,0:T(1,128)S(1)} %get-tuple-element.27), channel_id=1, source_target_pairs={{0,1},{1,2},{2,3},{4,5},{5,6},{6,7},{8,9},{9,10},{10,11},{12,13},{... | collective-permute-start | bytes 6152 | tf_op jit(solution)/shard_map/ppermute | solution.py:24
  4.4 73.5 %collective-permute-start.2 = (f32[1,512]{1,0:T(1,128)S(1)}, f32[1,512]{1,0:T(1,128)S(1)}, u32[]{:S(2)}, u32[]{:S(2)}) collective-permute-start(f32[1,512]{1,0:T(1,128)S(1)} %get-tuple-element.28), channel_id=1, source_target_pairs={{1,0},{2,1},{3,2},{5,4},{6,5},{7,6},{9,8},{10,9},{11,10},{13,12},{... | collective-permute-start | bytes 6152 | tf_op jit(solution)/shard_map/ppermute | solution.py:26
  5.8 72.0 %collective-permute-start.1 = (f32[256,1]{1,0:T(8,128)S(1)}, f32[256,1]{1,0:T(8,128)S(1)}, u32[]{:S(2)}, u32[]{:S(2)}) collective-permute-start(f32[256,1]{1,0:T(8,128)S(1)} %get-tuple-element.25), channel_id=1, source_target_pairs={{0,4},{4,8},{8,12},{12,16},{16,20},{20,24},{24,28},{28,0},{1,5},{5... | collective-permute-start | bytes 3080 | tf_op jit(solution)/shard_map/ppermute | solution.py:24
  8.1 69.7 %collective-permute-start = (f32[256,1]{1,0:T(8,128)S(1)}, f32[256,1]{1,0:T(8,128)S(1)}, u32[]{:S(2)}, u32[]{:S(2)}) collective-permute-start(f32[256,1]{1,0:T(8,128)S(1)} %get-tuple-element.26), channel_id=1, source_target_pairs={{4,0},{8,4},{12,8},{16,12},{20,16},{24,20},{28,24},{0,28},{5,1},{9... | collective-permute-start | bytes 3080 | tf_op jit(solution)/shard_map/ppermute | solution.py:26
  59.4 106.8 %collective-permute-start.11 = (f32[1,256]{1,0:T(1,128)S(1)}, f32[1,256]{1,0:T(1,128)S(1)}, u32[]{:S(2)}, u32[]{:S(2)}) collective-permute-start(f32[1,256]{1,0:T(1,128)S(1)} %get-tuple-element.49), channel_id=1, source_target_pairs={{0,1},{1,2},{2,3},{4,5},{5,6},{6,7},{8,9},{9,10},{10,11},{12,13},{... | collective-permute-start | bytes 3080 | tf_op jit(solution)/shard_map/ppermute | solution.py:24
  78.4 16.5 %collective-permute-start.6 = (f32[1,512]{1,0:T(1,128)S(1)}, f32[1,512]{1,0:T(1,128)S(1)}, u32[]{:S(2)}, u32[]{:S(2)}) collective-permute-start(f32[1,512]{1,0:T(1,128)S(1)} %get-tuple-element.23), channel_id=1, source_target_pairs={{1,0},{2,1},{3,2},{5,4},{6,5},{7,6},{9,8},{10,9},{11,10},{13,12},{... | collective-permute-start | bytes 6152 | tf_op jit(solution)/shard_map/ppermute | solution.py:26
  79.7 15.2 %collective-permute-start.7 = (f32[1,512]{1,0:T(1,128)S(1)}, f32[1,512]{1,0:T(1,128)S(1)}, u32[]{:S(2)}, u32[]{:S(2)}) collective-permute-start(f32[1,512]{1,0:T(1,128)S(1)} %get-tuple-element.24), channel_id=1, source_target_pairs={{0,1},{1,2},{2,3},{4,5},{5,6},{6,7},{8,9},{9,10},{10,11},{12,13},{... | collective-permute-start | bytes 6152 | tf_op jit(solution)/shard_map/ppermute | solution.py:24
  86.3 8.6 %collective-permute-start.5 = (f32[256,1]{1,0:T(8,128)S(1)}, f32[256,1]{1,0:T(8,128)S(1)}, u32[]{:S(2)}, u32[]{:S(2)}) collective-permute-start(f32[256,1]{1,0:T(8,128)S(1)} %get-tuple-element.22), channel_id=1, source_target_pairs={{0,4},{4,8},{8,12},{12,16},{16,20},{20,24},{24,28},{28,0},{1,5},{5... | collective-permute-start | bytes 3080 | tf_op jit(solution)/shard_map/ppermute | solution.py:24
  95.8 14.7 %collective-permute-start.14 = (f32[1,512]{1,0:T(1,128)S(1)}, f32[1,512]{1,0:T(1,128)S(1)}, u32[]{:S(2)}, u32[]{:S(2)}) collective-permute-start(f32[1,512]{1,0:T(1,128)S(1)} %get-tuple-element.19), channel_id=1, source_target_pairs={{1,0},{2,1},{3,2},{5,4},{6,5},{7,6},{9,8},{10,9},{11,10},{13,12},{... | collective-permute-start | bytes 6152 | tf_op jit(solution)/shard_map/ppermute | solution.py:26
  97.1 18.1 %collective-permute-start.15 = (f32[1,512]{1,0:T(1,128)S(1)}, f32[1,512]{1,0:T(1,128)S(1)}, u32[]{:S(2)}, u32[]{:S(2)}) collective-permute-start(f32[1,512]{1,0:T(1,128)S(1)} %get-tuple-element.20), channel_id=1, source_target_pairs={{0,1},{1,2},{2,3},{4,5},{5,6},{6,7},{8,9},{9,10},{10,11},{12,13},{... | collective-permute-start | bytes 6152 | tf_op jit(solution)/shard_map/ppermute | solution.py:24
  101.7 8.8 %collective-permute-start.13 = (f32[256,1]{1,0:T(8,128)S(1)}, f32[256,1]{1,0:T(8,128)S(1)}, u32[]{:S(2)}, u32[]{:S(2)}) collective-permute-start(f32[256,1]{1,0:T(8,128)S(1)} %get-tuple-element.18), channel_id=1, source_target_pairs={{0,4},{4,8},{8,12},{12,16},{16,20},{20,24},{24,28},{28,0},{1,5},{5... | collective-permute-start | bytes 3080 | tf_op jit(solution)/shard_map/ppermute | solution.py:24
  105.9 60.2 %collective-permute-start.10 = (f32[1,256]{1,0:T(1,128)S(1)}, f32[1,256]{1,0:T(1,128)S(1)}, u32[]{:S(2)}, u32[]{:S(2)}) collective-permute-start(f32[1,256]{1,0:T(1,128)S(1)} %get-tuple-element.50), channel_id=1, source_target_pairs={{1,0},{2,1},{3,2},{5,4},{6,5},{7,6},{9,8},{10,9},{11,10},{13,12},{... | collective-permute-start | bytes 3080 | tf_op jit(solution)/shard_map/ppermute | solution.py:26
  110.4 55.6 %collective-permute-start.9 = (f32[128,1]{1,0:T(8,128)S(1)}, f32[128,1]{1,0:T(8,128)S(1)}, u32[]{:S(2)}, u32[]{:S(2)}) collective-permute-start(f32[128,1]{1,0:T(8,128)S(1)} %get-tuple-element.47), channel_id=1, source_target_pairs={{0,4},{4,8},{8,12},{12,16},{16,20},{20,24},{24,28},{28,0},{1,5},{5... | collective-permute-start | bytes 1544 | tf_op jit(solution)/shard_map/ppermute | solution.py:24
  110.4 55.6 %collective-permute-start.8 = (f32[128,1]{1,0:T(8,128)S(1)}, f32[128,1]{1,0:T(8,128)S(1)}, u32[]{:S(2)}, u32[]{:S(2)}) collective-permute-start(f32[128,1]{1,0:T(8,128)S(1)} %get-tuple-element.48), channel_id=1, source_target_pairs={{4,0},{8,4},{12,8},{16,12},{20,16},{24,20},{28,24},{0,28},{5,1},{9... | collective-permute-start | bytes 1544 | tf_op jit(solution)/shard_map/ppermute | solution.py:26
  115.2 98.4 %collective-permute-start.23 = (f32[1,128]{1,0:T(1,128)}, f32[1,128]{1,0:T(1,128)}, u32[]{:S(2)}, u32[]{:S(2)}) collective-permute-start(f32[1,128]{1,0:T(1,128)} %get-tuple-element.79), channel_id=1, source_target_pairs={{0,1},{1,2},{2,3},{4,5},{5,6},{6,7},{8,9},{9,10},{10,11},{12,13},{... | collective-permute-start | bytes 1544 | tf_op jit(solution)/shard_map/ppermute | solution.py:24
  167.7 12.5 %collective-permute-start.18 = (f32[1,256]{1,0:T(1,128)}, f32[1,256]{1,0:T(1,128)S(1)}, u32[]{:S(2)}, u32[]{:S(2)}) collective-permute-start(f32[1,256]{1,0:T(1,128)} %get-tuple-element.45), channel_id=1, source_target_pairs={{1,0},{2,1},{3,2},{5,4},{6,5},{7,6},{9,8},{10,9},{11,10},{13,12},{... | collective-permute-start | bytes 3080 | tf_op jit(solution)/shard_map/ppermute | solution.py:26
  169.0 11.3 %collective-permute-start.19 = (f32[1,256]{1,0:T(1,128)}, f32[1,256]{1,0:T(1,128)S(1)}, u32[]{:S(2)}, u32[]{:S(2)}) collective-permute-start(f32[1,256]{1,0:T(1,128)} %get-tuple-element.46), channel_id=1, source_target_pairs={{0,1},{1,2},{2,3},{4,5},{5,6},{6,7},{8,9},{9,10},{10,11},{12,13},{... | collective-permute-start | bytes 3080 | tf_op jit(solution)/shard_map/ppermute | solution.py:24
  182.0 15.1 %collective-permute-start.26 = (f32[1,256]{1,0:T(1,128)S(1)}, f32[1,256]{1,0:T(1,128)S(1)}, u32[]{:S(2)}, u32[]{:S(2)}) collective-permute-start(f32[1,256]{1,0:T(1,128)S(1)} %get-tuple-element.41), channel_id=1, source_target_pairs={{1,0},{2,1},{3,2},{5,4},{6,5},{7,6},{9,8},{10,9},{11,10},{13,12},{... | collective-permute-start | bytes 3080 | tf_op jit(solution)/shard_map/ppermute | solution.py:26
  183.3 14.7 %collective-permute-start.27 = (f32[1,256]{1,0:T(1,128)S(1)}, f32[1,256]{1,0:T(1,128)S(1)}, u32[]{:S(2)}, u32[]{:S(2)}) collective-permute-start(f32[1,256]{1,0:T(1,128)S(1)} %get-tuple-element.42), channel_id=1, source_target_pairs={{0,1},{1,2},{2,3},{4,5},{5,6},{6,7},{8,9},{9,10},{10,11},{12,13},{... | collective-permute-start | bytes 3080 | tf_op jit(solution)/shard_map/ppermute | solution.py:24
  190.8 22.8 %collective-permute-start.22 = (f32[1,128]{1,0:T(1,128)}, f32[1,128]{1,0:T(1,128)S(1)}, u32[]{:S(2)}, u32[]{:S(2)}) collective-permute-start(f32[1,128]{1,0:T(1,128)} %get-tuple-element.80), channel_id=1, source_target_pairs={{1,0},{2,1},{3,2},{5,4},{6,5},{7,6},{9,8},{10,9},{11,10},{13,12},{... | collective-permute-start | bytes 1544 | tf_op jit(solution)/shard_map/ppermute | solution.py:26
  196.0 17.5 %collective-permute-start.20 = (f32[64,1]{1,0:T(8,128)}, f32[64,1]{1,0:T(8,128)S(1)}, u32[]{:S(2)}, u32[]{:S(2)}) collective-permute-start(f32[64,1]{1,0:T(8,128)} %get-tuple-element.77), channel_id=1, source_target_pairs={{4,0},{8,4},{12,8},{16,12},{20,16},{24,20},{28,24},{0,28},{5,1},{9... | collective-permute-start | bytes 776 | tf_op jit(solution)/shard_map/ppermute | solution.py:26
  197.1 16.4 %collective-permute-start.21 = (f32[64,1]{1,0:T(8,128)}, f32[64,1]{1,0:T(8,128)S(1)}, u32[]{:S(2)}, u32[]{:S(2)}) collective-permute-start(f32[64,1]{1,0:T(8,128)} %get-tuple-element.78), channel_id=1, source_target_pairs={{0,4},{4,8},{8,12},{12,16},{16,20},{20,24},{24,28},{28,0},{1,5},{5... | collective-permute-start | bytes 776 | tf_op jit(solution)/shard_map/ppermute | solution.py:24
  214.4 15.0 %collective-permute-start.30 = (f32[1,128]{1,0:T(1,128)S(1)}, f32[1,128]{1,0:T(1,128)S(1)}, u32[]{:S(2)}, u32[]{:S(2)}) collective-permute-start(f32[1,128]{1,0:T(1,128)S(1)} %get-tuple-element.75), channel_id=1, source_target_pairs={{1,0},{2,1},{3,2},{5,4},{6,5},{7,6},{9,8},{10,9},{11,10},{13,12},{... | collective-permute-start | bytes 1544 | tf_op jit(solution)/shard_map/ppermute | solution.py:26
  215.7 13.7 %collective-permute-start.31 = (f32[1,128]{1,0:T(1,128)S(1)}, f32[1,128]{1,0:T(1,128)S(1)}, u32[]{:S(2)}, u32[]{:S(2)}) collective-permute-start(f32[1,128]{1,0:T(1,128)S(1)} %get-tuple-element.76), channel_id=1, source_target_pairs={{0,1},{1,2},{2,3},{4,5},{5,6},{6,7},{8,9},{9,10},{10,11},{12,13},{... | collective-permute-start | bytes 1544 | tf_op jit(solution)/shard_map/ppermute | solution.py:24
  223.4 29.7 %collective-permute-start.34 = (f32[1,64]{1,0:T(1,128)}, f32[1,64]{1,0:T(1,128)}, u32[]{:S(2)}, u32[]{:S(2)}) collective-permute-start(f32[1,64]{1,0:T(1,128)} %get-tuple-element.91), channel_id=1, source_target_pairs={{1,0},{2,1},{3,2},{5,4},{6,5},{7,6},{9,8},{10,9},{11,10},{13,12},{... | collective-permute-start | bytes 776 | tf_op jit(solution)/shard_map/ppermute | solution.py:26
  230.2 12.9 %collective-permute-start.38 = (f32[1,128]{1,0:T(1,128)S(1)}, f32[1,128]{1,0:T(1,128)S(1)}, u32[]{:S(2)}, u32[]{:S(2)}) collective-permute-start(f32[1,128]{1,0:T(1,128)S(1)} %get-tuple-element.71), channel_id=1, source_target_pairs={{1,0},{2,1},{3,2},{5,4},{6,5},{7,6},{9,8},{10,9},{11,10},{13,12},{... | collective-permute-start | bytes 1544 | tf_op jit(solution)/shard_map/ppermute | solution.py:26
  231.5 16.3 %collective-permute-start.39 = (f32[1,128]{1,0:T(1,128)S(1)}, f32[1,128]{1,0:T(1,128)S(1)}, u32[]{:S(2)}, u32[]{:S(2)}) collective-permute-start(f32[1,128]{1,0:T(1,128)S(1)} %get-tuple-element.72), channel_id=1, source_target_pairs={{0,1},{1,2},{2,3},{4,5},{5,6},{6,7},{8,9},{9,10},{10,11},{12,13},{... | collective-permute-start | bytes 1544 | tf_op jit(solution)/shard_map/ppermute | solution.py:24
  238.9 14.1 %collective-permute-start.35 = (f32[1,64]{1,0:T(1,128)}, f32[1,64]{1,0:T(1,128)}, u32[]{:S(2)}, u32[]{:S(2)}) collective-permute-start(f32[1,64]{1,0:T(1,128)} %get-tuple-element.92), channel_id=1, source_target_pairs={{0,1},{1,2},{2,3},{4,5},{5,6},{6,7},{8,9},{9,10},{10,11},{12,13},{... | collective-permute-start | bytes 776 | tf_op jit(solution)/shard_map/ppermute | solution.py:24
  243.1 9.9 %collective-permute-start.33 = (f32[32,1]{1,0:T(8,128)}, f32[32,1]{1,0:T(8,128)}, u32[]{:S(2)}, u32[]{:S(2)}) collective-permute-start(f32[32,1]{1,0:T(8,128)} %get-tuple-element.89), channel_id=1, source_target_pairs={{0,4},{4,8},{8,12},{12,16},{16,20},{20,24},{24,28},{28,0},{1,5},{5... | collective-permute-start | bytes 392 | tf_op jit(solution)/shard_map/ppermute | solution.py:24
  243.1 9.9 %collective-permute-start.32 = (f32[32,1]{1,0:T(8,128)}, f32[32,1]{1,0:T(8,128)}, u32[]{:S(2)}, u32[]{:S(2)}) collective-permute-start(f32[32,1]{1,0:T(8,128)} %get-tuple-element.90), channel_id=1, source_target_pairs={{4,0},{8,4},{12,8},{16,12},{20,16},{24,20},{28,24},{0,28},{5,1},{9... | collective-permute-start | bytes 392 | tf_op jit(solution)/shard_map/ppermute | solution.py:26
  254.0 14.2 %collective-permute-start.40 = (f32[1,32,2]{2,1,0:T(8,128)S(1)}, f32[1,32,2]{2,1,0:T(8,128)S(1)}, u32[]{:S(2)}, u32[]{:S(2)}) collective-permute-start(f32[1,32,2]{2,1,0:T(8,128)S(1)} %get-tuple-element.87), channel_id=1, source_target_pairs={{0,4},{4,8},{8,12},{12,16},{16,20},{20,24},{24,28},{28,0},{1,5},{5... | collective-permute-start | bytes 776 | tf_op jit(solution)/shard_map/ppermute | solution.py:24
  254.0 14.2 %collective-permute-start.41 = (f32[1,32,2]{2,1,0:T(8,128)S(1)}, f32[1,32,2]{2,1,0:T(8,128)S(1)}, u32[]{:S(2)}, u32[]{:S(2)}) collective-permute-start(f32[1,32,2]{2,1,0:T(8,128)S(1)} %get-tuple-element.88), channel_id=1, source_target_pairs={{4,0},{8,4},{12,8},{16,12},{20,16},{24,20},{28,24},{0,28},{5,1},{9... | collective-permute-start | bytes 776 | tf_op jit(solution)/shard_map/ppermute | solution.py:26
  268.2 9.4 %collective-permute-start.42 = (f32[1,2,68]{2,1,0:T(2,128)S(1)}, f32[1,2,68]{2,1,0:T(2,128)S(1)}, u32[]{:S(2)}, u32[]{:S(2)}) collective-permute-start(f32[1,2,68]{2,1,0:T(2,128)S(1)} %get-tuple-element.59), channel_id=1, source_target_pairs={{0,1},{1,2},{2,3},{4,5},{5,6},{6,7},{8,9},{9,10},{10,11},{12,13},{... | collective-permute-start | bytes 1640 | tf_op jit(solution)/shard_map/ppermute | solution.py:24
  328.5 17.6 %collective-permute-start.62 = (f32[1,128]{1,0:T(1,128)S(1)}, f32[1,128]{1,0:T(1,128)S(1)}, u32[]{:S(2)}, u32[]{:S(2)}) collective-permute-start(f32[1,128]{1,0:T(1,128)S(1)} %get-tuple-element.67), channel_id=1, source_target_pairs={{1,0},{2,1},{3,2},{5,4},{6,5},{7,6},{9,8},{10,9},{11,10},{13,12},{... | collective-permute-start | bytes 1544 | tf_op jit(solution)/shard_map/ppermute | solution.py:26
  329.8 16.3 %collective-permute-start.63 = (f32[1,128]{1,0:T(1,128)S(1)}, f32[1,128]{1,0:T(1,128)S(1)}, u32[]{:S(2)}, u32[]{:S(2)}) collective-permute-start(f32[1,128]{1,0:T(1,128)S(1)} %get-tuple-element.68), channel_id=1, source_target_pairs={{0,1},{1,2},{2,3},{4,5},{5,6},{6,7},{8,9},{9,10},{10,11},{12,13},{... | collective-permute-start | bytes 1544 | tf_op jit(solution)/shard_map/ppermute | solution.py:24
  347.2 11.1 %collective-permute-start.66 = (f32[1,128]{1,0:T(1,128)S(1)}, f32[1,128]{1,0:T(1,128)S(1)}, u32[]{:S(2)}, u32[]{:S(2)}) collective-permute-start(f32[1,128]{1,0:T(1,128)S(1)} %get-tuple-element.63), channel_id=1, source_target_pairs={{1,0},{2,1},{3,2},{5,4},{6,5},{7,6},{9,8},{10,9},{11,10},{13,12},{... | collective-permute-start | bytes 1544 | tf_op jit(solution)/shard_map/ppermute | solution.py:26
  348.5 9.8 %collective-permute-start.67 = (f32[1,128]{1,0:T(1,128)S(1)}, f32[1,128]{1,0:T(1,128)S(1)}, u32[]{:S(2)}, u32[]{:S(2)}) collective-permute-start(f32[1,128]{1,0:T(1,128)S(1)} %get-tuple-element.64), channel_id=1, source_target_pairs={{0,1},{1,2},{2,3},{4,5},{5,6},{6,7},{8,9},{9,10},{10,11},{12,13},{... | collective-permute-start | bytes 1544 | tf_op jit(solution)/shard_map/ppermute | solution.py:24
  370.3 11.6 %collective-permute-start.70 = (f32[1,256]{1,0:T(1,128)S(1)}, f32[1,256]{1,0:T(1,128)S(1)}, u32[]{:S(2)}, u32[]{:S(2)}) collective-permute-start(f32[1,256]{1,0:T(1,128)S(1)} %get-tuple-element.37), channel_id=1, source_target_pairs={{1,0},{2,1},{3,2},{5,4},{6,5},{7,6},{9,8},{10,9},{11,10},{13,12},{... | collective-permute-start | bytes 3080 | tf_op jit(solution)/shard_map/ppermute | solution.py:26
  371.6 10.3 %collective-permute-start.71 = (f32[1,256]{1,0:T(1,128)S(1)}, f32[1,256]{1,0:T(1,128)S(1)}, u32[]{:S(2)}, u32[]{:S(2)}) collective-permute-start(f32[1,256]{1,0:T(1,128)S(1)} %get-tuple-element.38), channel_id=1, source_target_pairs={{0,1},{1,2},{2,3},{4,5},{5,6},{6,7},{8,9},{9,10},{10,11},{12,13},{... | collective-permute-start | bytes 3080 | tf_op jit(solution)/shard_map/ppermute | solution.py:24
  382.2 11.5 %collective-permute-start.74 = (f32[1,256]{1,0:T(1,128)S(1)}, f32[1,256]{1,0:T(1,128)S(1)}, u32[]{:S(2)}, u32[]{:S(2)}) collective-permute-start(f32[1,256]{1,0:T(1,128)S(1)} %get-tuple-element.33), channel_id=1, source_target_pairs={{1,0},{2,1},{3,2},{5,4},{6,5},{7,6},{9,8},{10,9},{11,10},{13,12},{... | collective-permute-start | bytes 3080 | tf_op jit(solution)/shard_map/ppermute | solution.py:26
  383.5 10.2 %collective-permute-start.75 = (f32[1,256]{1,0:T(1,128)S(1)}, f32[1,256]{1,0:T(1,128)S(1)}, u32[]{:S(2)}, u32[]{:S(2)}) collective-permute-start(f32[1,256]{1,0:T(1,128)S(1)} %get-tuple-element.34), channel_id=1, source_target_pairs={{0,1},{1,2},{2,3},{4,5},{5,6},{6,7},{8,9},{9,10},{10,11},{12,13},{... | collective-permute-start | bytes 3080 | tf_op jit(solution)/shard_map/ppermute | solution.py:24
  429.7 13.2 %collective-permute-start.78 = (f32[1,512]{1,0:T(1,128)S(1)}, f32[1,512]{1,0:T(1,128)S(1)}, u32[]{:S(2)}, u32[]{:S(2)}) collective-permute-start(f32[1,512]{1,0:T(1,128)S(1)} %get-tuple-element.15), channel_id=1, source_target_pairs={{1,0},{2,1},{3,2},{5,4},{6,5},{7,6},{9,8},{10,9},{11,10},{13,12},{... | collective-permute-start | bytes 6152 | tf_op jit(solution)/shard_map/ppermute | solution.py:26
  431.0 11.9 %collective-permute-start.79 = (f32[1,512]{1,0:T(1,128)S(1)}, f32[1,512]{1,0:T(1,128)S(1)}, u32[]{:S(2)}, u32[]{:S(2)}) collective-permute-start(f32[1,512]{1,0:T(1,128)S(1)} %get-tuple-element.16), channel_id=1, source_target_pairs={{0,1},{1,2},{2,3},{4,5},{5,6},{6,7},{8,9},{9,10},{10,11},{12,13},{... | collective-permute-start | bytes 6152 | tf_op jit(solution)/shard_map/ppermute | solution.py:24
  443.7 13.0 %collective-permute-start.82 = (f32[1,512]{1,0:T(1,128)S(1)}, f32[1,512]{1,0:T(1,128)S(1)}, u32[]{:S(2)}, u32[]{:S(2)}) collective-permute-start(f32[1,512]{1,0:T(1,128)S(1)} %get-tuple-element.11), channel_id=1, source_target_pairs={{1,0},{2,1},{3,2},{5,4},{6,5},{7,6},{9,8},{10,9},{11,10},{13,12},{... | collective-permute-start | bytes 6152 | tf_op jit(solution)/shard_map/ppermute | solution.py:26
  445.0 11.7 %collective-permute-start.83 = (f32[1,512]{1,0:T(1,128)S(1)}, f32[1,512]{1,0:T(1,128)S(1)}, u32[]{:S(2)}, u32[]{:S(2)}) collective-permute-start(f32[1,512]{1,0:T(1,128)S(1)} %get-tuple-element.12), channel_id=1, source_target_pairs={{0,1},{1,2},{2,3},{4,5},{5,6},{6,7},{8,9},{9,10},{10,11},{12,13},{... | collective-permute-start | bytes 6152 | tf_op jit(solution)/shard_map/ppermute | solution.py:24
  457.5 13.3 %collective-permute-start.86 = (f32[1,512]{1,0:T(1,128)S(1)}, f32[1,512]{1,0:T(1,128)S(1)}, u32[]{:S(2)}, u32[]{:S(2)}) collective-permute-start(f32[1,512]{1,0:T(1,128)S(1)} %get-tuple-element.7), channel_id=1, source_target_pairs={{1,0},{2,1},{3,2},{5,4},{6,5},{7,6},{9,8},{10,9},{11,10},{13,12},{... | collective-permute-start | bytes 6152 | tf_op jit(solution)/shard_map/ppermute | solution.py:26
  458.8 12.0 %collective-permute-start.87 = (f32[1,512]{1,0:T(1,128)S(1)}, f32[1,512]{1,0:T(1,128)S(1)}, u32[]{:S(2)}, u32[]{:S(2)}) collective-permute-start(f32[1,512]{1,0:T(1,128)S(1)} %get-tuple-element.8), channel_id=1, source_target_pairs={{0,1},{1,2},{2,3},{4,5},{5,6},{6,7},{8,9},{9,10},{10,11},{12,13},{... | collective-permute-start | bytes 6152 | tf_op jit(solution)/shard_map/ppermute | solution.py:24
  462.2 8.6 %collective-permute-start.85 = (f32[256,1]{1,0:T(8,128)S(1)}, f32[256,1]{1,0:T(8,128)S(1)}, u32[]{:S(2)}, u32[]{:S(2)}) collective-permute-start(f32[256,1]{1,0:T(8,128)S(1)} %get-tuple-element.6), channel_id=1, source_target_pairs={{0,4},{4,8},{8,12},{12,16},{16,20},{20,24},{24,28},{28,0},{1,5},{5... | collective-permute-start | bytes 3080 | tf_op jit(solution)/shard_map/ppermute | solution.py:24
  (68 other events, 1093.2 us)
where the time goes:
time: 475 us; the launch traced here: 472 us
  starting transfers between devices  173 us (36%)
  local copies, waits for them, and re-layouts  149 us (31%)
  waiting for transfers between devices  84.1 us (18%)
  other arithmetic  63.9 us (13%)
    ppermute x44, starting transfers between devices, with_halo(): lax.ppermute(tail, axis, [(i, (i + 1) % count) for i in range(ends)])  89.1 us
    ppermute x44, starting transfers between devices, with_halo(): lax.ppermute(head, axis, [((i + 1) % count, i) for i in range(ends)])  84.1 us
    reshape x4, local copies, waits for them, and re-layouts, restrict(): return field.reshape(row_count // 2, 2, col_count // 2, 2).mean(axis=(1, 3))  82.3 us
    ppermute x44, waiting for transfers between devices, with_halo(): lax.ppermute(tail, axis, [(i, (i + 1) % count) for i in range(ends)])  46.5 us
    ppermute x44, waiting for transfers between devices, with_halo(): lax.ppermute(head, axis, [((i + 1) % count, i) for i in range(ends)])  37.6 us
    reduce_sum x6, other arithmetic, restrict(): return field.reshape(row_count // 2, 2, col_count // 2, 2).mean(axis=(1, 3))  37.5 us
    reshape x3, local copies, waits for them, and re-layouts, prolong(): jnp.broadcast_to(field[:, None, :, None], (row_count, 2, col_count, 2))  33 us
    broadcast_in_dim x3, local copies, waits for them, and re-layouts, prolong(): jnp.broadcast_to(field[:, None, :, None], (row_count, 2, col_count, 2))  15.7 us
  transfers between devices with their start and end apart: 88, of which 31 were waited for; matrix products, arithmetic and copies ran while one was open for 32% of the time, Pallas kernels for 0%

commit v1 on v0

v1 whole, which is shorter than its diff:
```python
import functools

import jax
import jax.numpy as jnp
from jax import lax
from jax.experimental import pallas as pl
from jax.experimental.pallas import tpu as pltpu
from jax.sharding import PartitionSpec as P

DEPTH_LEVELS = 50
COARSE_SWEEPS = 9
OMEGA = 0.8
SIGMA = 1e-05
HALO = 16
DEEP = 24
DEEP_LANES = 32
MESH = pl.DeviceIdType.MESH
F32 = jnp.float32
BF16 = jnp.bfloat16


def lanes_of(shape=(8, 128)):
    return lax.broadcasted_iota(jnp.int32, shape, 1)


def east_of(tiles):
    if len(tiles) == 1:
        return [pltpu.roll(tiles[0], 127, 1)]
    lane = lanes_of()
    turned = [pltpu.roll(x, 127, 1) for x in tiles]
    return [jnp.where(lane == 127, turned[(t + 1) % len(tiles)], turned[t]) for t in range(len(tiles))]


def west_of(tiles):
    if len(tiles) == 1:
        return [pltpu.roll(tiles[0], 1, 1)]
    lane = lanes_of()
    turned = [pltpu.roll(x, 1, 1) for x in tiles]
    return [jnp.where(lane == 0, turned[t - 1], turned[t]) for t in range(len(tiles))]


def upper(x):
    return pltpu.roll(x, 7, 0)


def lower(x):
    return pltpu.roll(x, 1, 0)


def at(j):
    start = (j + 1) * 8
    return pl.ds(start if isinstance(start, int) else pl.multiple_of(start, 8), 8)


def load(ref, j):
    return [ref[t, at(j), :] for t in range(ref.shape[0])]


def store(ref, j, tiles):
    for t, x in enumerate(tiles):
        ref[t, at(j), :] = x


def each(count, unroll, body):
    if unroll >= count:
        for j in range(count):
            body(j)
    else:
        lax.fori_loop(0, count, lambda j, c: (body(j), c)[1], 0, unroll=unroll)


def wrap(ref, count):
    store(ref, -1, [lower(x) for x in load(ref, count - 1)])
    store(ref, count, [upper(x) for x in load(ref, 0)])


def split_dot(x, mat, parts):
    total = None
    for part in range(parts):
        piece = x.astype(BF16)
        term = jnp.dot(piece, mat, preferred_element_type=F32)
        total = term if total is None else total + term
        if part < parts - 1:
            x = x - piece.astype(F32)
    return total


def shrink(tiles, mats, parts):
    outs = []
    for p in range(len(tiles) // 2):
        outs.append(split_dot(tiles[2 * p], mats[0], parts) + split_dot(tiles[2 * p + 1], mats[1], parts))
    if len(tiles) % 2:
        outs.append(split_dot(tiles[-1], mats[2], parts))
    return outs


def spread(tiles, mats, fine_count, parts):
    outs = []
    for p in range(fine_count // 2):
        outs += [split_dot(tiles[p], mats[3], parts), split_dot(tiles[p], mats[4], parts)]
    if fine_count % 2:
        outs.append(split_dot(tiles[fine_count // 2], mats[5], parts))
    return outs


class Level:
    def __init__(self, index, count, unroll, refs):
        self.scale = 0.0625**index / DEPTH_LEVELS
        self.count, self.unroll = count, unroll
        self.h, self.s, self.ke, self.kn, self.w, self.d, self.a, self.b, self.half = refs

    def coefficients(self):
        wrap(self.h, self.count)

        def body(j):
            h = load(self.h, j)
            ke = [jnp.minimum(x, y) * self.scale for x, y in zip(h, east_of(h))]
            kw = west_of(ke)
            kn = [jnp.minimum(x, y) * self.scale for x, y in zip(h, load(self.h, j + 1))]
            ks = [jnp.minimum(x, y) * self.scale for x, y in zip(h, load(self.h, j - 1))]
            faces = [a + b + c + d for a, b, c, d in zip(ke, kw, kn, ks)]
            diag = [SIGMA + f for f in faces]
            w = [OMEGA / d for d in diag]
            s = [jnp.where(f > 0.0, x, 0.0) for f, x in zip(faces, load(self.s, j))]
            for ref, value in ((self.ke, ke), (self.kn, kn), (self.w, w), (self.d, diag), (self.s, s)):
                store(ref, j, value)
            store(self.a, j, [x * y for x, y in zip(w, s)])

        each(self.count, self.unroll, body)
        wrap(self.kn, self.count)

    def pulled(self, ref, j):
        v, ke = load(ref, j), load(self.ke, j)
        flow = west_of([x * y for x, y in zip(ke, v)])
        rows = zip(ke, east_of(v), flow, load(self.kn, j), load(ref, j + 1), load(self.kn, j - 1), load(ref, j - 1))
        return v, [k * e + f + n * vn + s * vs for k, e, f, n, vn, s, vs in rows]

    def sweep(self, src, dst):
        wrap(src, self.count)

        def body(j):
            v, acc = self.pulled(src, j)
            new = [(1.0 - OMEGA) * x + w * (s + a) for x, w, s, a in zip(v, load(self.w, j), load(self.s, j), acc)]
            store(dst, j, new)

        each(self.count, self.unroll, body)

    def residual(self, ref, j):
        v, acc = self.pulled(ref, j)
        return [s - d * x + a for s, d, x, a in zip(load(self.s, j), load(self.d, j), v, acc)]

    def halve(self, rows_of, factor):
        def body(j):
            for t, (x, y) in enumerate(zip(rows_of(2 * j), rows_of(2 * j + 1))):
                start = j * 8 if isinstance(j, int) else pl.multiple_of(j * 8, 8)
                self.half[t, pl.ds(start, 8), :] = (x + y) * factor

        each(self.count // 2, self.unroll // 2, body)

    def down(self):
        self.coefficients()
        self.sweep(self.a, self.b)
        wrap(self.b, self.count)
        self.halve(lambda j: self.residual(self.b, j), 0.25)

    def up(self):
        def body(j):
            start = j * 8 if isinstance(j, int) else pl.multiple_of(j * 8, 8)
            extra = [self.half[t, pl.ds(start, 8), :] for t in range(self.half.shape[0])]
            for i in (2 * j, 2 * j + 1):
                store(self.b, i, [x + y for x, y in zip(load(self.b, i), extra)])

        each(self.count // 2, self.unroll // 2, body)
        self.sweep(self.b, self.a)
        self.sweep(self.a, self.b)


class Exchange:
    def __init__(self, x, halo, width, refs, sems):
        self.x, self.halo, self.width = x, halo, width
        self.pack, self.got, self.corner = refs
        self.sems = sems
        self.tiles = x.shape[1] - 1
        self.n = x.shape[2] - 2 * halo
        self.groups = 128 // width

    def fill(self, f):
        lane = lanes_of()
        for side in range(2):
            for m in range(self.n // 8 // self.groups):
                total = None
                for g in range(self.groups):
                    row = self.halo + 8 * (m * self.groups + g)
                    chunk = self.x[f, 0 if side == 0 else self.tiles - 1, row : row + 8, :]
                    shift = (self.width * g + side * self.width) % 128
                    chunk = pltpu.roll(chunk, shift, 1) if shift else chunk
                    total = chunk if total is None else jnp.where(lane >= self.width * g, chunk, total)
                self.pack[side, f, 8 * m : 8 * m + 8, :] = total

    def start(self, place):
        lat, lon, nlat, nlon = place
        copies = []

        def send(src, dst, dlat, dlon):
            k = len(copies)
            copy = pltpu.make_async_remote_copy(
                src_ref=src,
                dst_ref=dst,
                send_sem=self.sems.at[0, k],
                recv_sem=self.sems.at[1, k],
                device_id={"lat": lax.rem(lat + dlat + nlat, nlat), "lon": lax.rem(lon + dlon + nlon, nlon)},
                device_id_type=MESH,
            )
            copy.start()
            copies.append(copy)

        h, n, last = self.halo, self.n, self.pack.shape[2] - 8
        for side, dlon in ((0, -1), (1, 1)):
            send(self.pack.at[side], self.got.at[side], 0, dlon)
        for side, dlon in ((0, -1), (1, 1)):
            send(self.pack.at[side, :, pl.ds(last, 8), :], self.corner.at[side], 1, dlon)
            send(self.pack.at[side, :, pl.ds(0, 8), :], self.corner.at[2 + side], -1, dlon)
        core = pl.ds(0, self.tiles)
        send(self.x.at[:, core, pl.ds(n, h), :], self.x.at[:, core, pl.ds(0, h), :], 1, 0)
        send(self.x.at[:, core, pl.ds(h, h), :], self.x.at[:, core, pl.ds(h + n, h), :], -1, 0)
        self.copies = copies

    def finish(self, place):
        lat, lon, nlat, nlon = place
        for copy in self.copies:
            copy.wait()
        lane = lanes_of()
        edge, total = self.halo // 8, self.x.shape[2] // 8
        count = self.n // 8
        for f in range(2):
            for b in range(total):
                a = b - edge
                if a < 0:
                    a, refs = a + count, (self.corner.at[0, f], self.corner.at[1, f])
                    start = 0
                elif a >= count:
                    a, refs = a - count, (self.corner.at[2, f], self.corner.at[3, f])
                    start = 0
                else:
                    start = 8 * (a // self.groups)
                    refs = (self.got.at[0, f], self.got.at[1, f])
                g = a % self.groups
                east, west = refs[0][start : start + 8, :], refs[1][start : start + 8, :]
                shift = (128 - self.width * g) % 128
                east = pltpu.roll(east, shift, 1) if shift else east
                shift = (256 - self.width - self.width * g) % 128
                west = pltpu.roll(west, shift, 1) if shift else west
                tile = jnp.where(lane < self.width, east, jnp.where(lane >= 128 - self.width, west, 0.0))
                self.x[f, self.tiles, 8 * b : 8 * b + 8, :] = tile
        for blocks, pole in ((range(edge), lat == 0), (range(total - edge, total), lat == nlat - 1)):
            keep = jnp.where(pole, 0.0, 1.0)
            for f in range(2):
                for t in range(self.tiles + 1):
                    for b in blocks:
                        self.x[f, t, 8 * b : 8 * b + 8, :] = self.x[f, t, 8 * b : 8 * b + 8, :] * keep


def kernel(place_of, right_hbm, depth_hbm, mask_hbm, press_hbm, resid_hbm, x0, depth, mask, mats, x2, y2, z2, c1, *rest):
    nlat, nlon = place_of
    pack0, got0, corner0, pack2, got2, corner2, sems0, sems2, in_sems, out_sems = rest[:10]
    refs0, refs1, refs2 = rest[10:19], rest[19:28], rest[28:37]
    lat, lon = lax.axis_index("lat"), lax.axis_index("lon")
    place = (lat, lon, nlat, nlon)
    rows = depth.shape[1]
    tiles = depth.shape[0]

    loads = []
    for t in range(tiles):
        cols = pl.ds(128 * t, 128)
        for i, (src, dst) in enumerate(
            (
                (depth_hbm.at[:, cols], depth.at[t]),
                (mask_hbm.at[:, cols], mask.at[t]),
                (right_hbm.at[:, cols], x0.at[1, t, pl.ds(HALO, rows), :]),
            )
        ):
            loads.append(pltpu.make_async_copy(src, dst, in_sems.at[i, t]))
            loads[-1].start()

    barrier = pltpu.get_barrier_semaphore()
    for dlat in (-1, 0, 1):
        for dlon in (-1, 0, 1):
            if dlat or dlon:
                pl.semaphore_signal(
                    barrier,
                    inc=1,
                    device_id={"lat": lax.rem(lat + dlat + nlat, nlat), "lon": lax.rem(lon + dlon + nlon, nlon)},
                    device_id_type=MESH,
                )

    fine = lax.broadcasted_iota(jnp.int32, (128, 128), 0)
    coarse = lanes_of((128, 128))
    for base, f, c in ((0, fine, coarse), (3, coarse, fine)):
        first = jnp.right_shift(f, 1)
        for i, target in enumerate((first, first + 64, jnp.where(f < 64, first, first + 64))):
            mats[base + i] = jnp.where(target == c, 1.0, 0.0).astype(BF16)
    mats = [mats[i] for i in range(6)]

    for copy in loads:
        copy.wait()
    for t in range(tiles):
        x0[0, t, HALO : HALO + rows, :] = (depth[t] * mask[t]).astype(F32)
    outer = Exchange(x0, HALO, HALO, (pack0, got0, corner0), sems0)
    outer.fill(0)
    outer.fill(1)
    pl.semaphore_wait(barrier, 8)
    outer.start(place)
    outer.finish(place)

    count0 = refs0[0].shape[1] // 8 - 2
    count1 = refs1[0].shape[1] // 8 - 2
    count2 = refs2[0].shape[1] // 8 - 2
    level0 = Level(0, count0, 4, refs0)
    level1 = Level(1, count1, 6, refs1)
    level2 = Level(2, count2, count2, refs2)
    for j in range(count0):
        for t in range(tiles + 1):
            level0.h[t, at(j), :] = x0[0, t, pl.ds(j, 8, stride=count0), :]
            level0.s[t, at(j), :] = x0[1, t, pl.ds(j, 8, stride=count0), :]

    level0.halve(lambda j: load(level0.h, j), 1.0)
    for t, x in enumerate(shrink([level0.half[t] for t in range(tiles + 1)], mats, 1)):
        level1.h[t, 8 : 8 + 8 * count1, :] = x
    level0.down()
    for t, x in enumerate(shrink([level0.half[t] for t in range(tiles + 1)], mats, 3)):
        level1.s[t, 8 : 8 + 8 * count1, :] = x

    half1 = count1 // 2
    margin = HALO // 4
    deep_rows = x2.shape[2] - 2 * DEEP

    def pass_down(f, parts):
        out = shrink([level1.half[0], level1.half[1]], mats, parts)[0]
        for j in range(half1):
            y2[pl.ds(j, 8, stride=half1), :] = out[8 * j : 8 * j + 8]
        for a in range(deep_rows // 8):
            x2[f, 0, DEEP + 8 * a : DEEP + 8 * a + 8, :] = y2[margin + 8 * a : margin + 8 * a + 8, :]

    level1.halve(lambda j: load(level1.h, j), 1.0)
    pass_down(0, 2)
    level1.down()
    pass_down(1, 3)

    inner = Exchange(x2, DEEP, DEEP_LANES, (pack2, got2, corner2), sems2)
    inner.fill(0)
    inner.fill(1)
    inner.start(place)
    inner.finish(place)
    for j in range(count2):
        for t in range(2):
            level2.h[t, at(j), :] = x2[0, t, pl.ds(j, 8, stride=count2), :]
            level2.s[t, at(j), :] = x2[1, t, pl.ds(j, 8, stride=count2), :]
    count3 = count2 // 2
    level2.halve(lambda j: load(level2.h, j), 1.0)
    height = shrink([level2.half[0], level2.half[1]], mats, 2)[0]
    level2.down()
    source = shrink([level2.half[0], level2.half[1]], mats, 3)[0]

    scale = 0.0625**3 / DEPTH_LEVELS
    h = [height[8 * j : 8 * j + 8] for j in range(count3)]
    s = [source[8 * j : 8 * j + 8] for j in range(count3)]

    def north(v):
        return v[1:] + [upper(v[0])]

    ke = [jnp.minimum(x, pltpu.roll(x, 127, 1)) * scale for x in h]
    kn = [jnp.minimum(x, y) * scale for x, y in zip(h, north(h))]
    ks = [lower(kn[-1])] + kn[:-1]
    faces = [a + pltpu.roll(a, 1, 1) + b + c for a, b, c in zip(ke, kn, ks)]
    w = [OMEGA / (SIGMA + f) for f in faces]
    s = [jnp.where(f > 0.0, x, 0.0) for f, x in zip(faces, s)]
    v = [x * y for x, y in zip(w, s)]
    for _ in range(COARSE_SWEEPS - 1):
        up, down = north(v), [lower(v[-1])] + v[:-1]
        v = [
            (1.0 - OMEGA) * v[j]
            + w[j]
            * (s[j] + ke[j] * pltpu.roll(v[j], 127, 1) + pltpu.roll(ke[j] * v[j], 1, 1) + kn[j] * up[j] + ks[j] * down[j])
            for j in range(count3)
        ]

    for t, x in enumerate(spread([jnp.concatenate(v, axis=0)], mats, 2, 3)):
        level2.half[t] = x
    level2.up()
    for j in range(count2):
        for t in range(2):
            z2[t, pl.ds(j, 8, stride=count2), :] = level2.b[t, at(j), :]
    for j in range(half1):
        for t in range(2):
            c1[t, 8 * j : 8 * j + 8, :] = z2[t, pl.ds(DEEP - margin + j, 8, stride=half1), :]
    for t, x in enumerate(spread([c1[0], c1[1]], mats, 3, 3)):
        level1.half[t] = x
    level1.up()
    body = pl.ds(8, 8 * count1)
    for t, x in enumerate(spread([level1.b[t, body, :] for t in range(3)], mats, tiles + 1, 3)):
        level0.half[t] = x
    level0.up()
    wrap(level0.b, count0)
    each(count0, 4, lambda j: store(level0.a, j, level0.residual(level0.b, j)))

    stores = []
    for i, (ref, out) in enumerate(((level0.b, press_hbm), (level0.a, resid_hbm))):
        for t in range(tiles):
            for j in range(count0):
                x0[i, t, pl.ds(j, 8, stride=count0), :] = ref[t, at(j), :]
            stores.append(
                pltpu.make_async_copy(
                    x0.at[i, t, pl.ds(HALO, rows), :], out.at[:, pl.ds(128 * t, 128)], out_sems.at[i, t]
                )
            )
            stores[-1].start()
    for copy in stores:
        copy.wait()


def solution(mesh):
    nlat, nlon = mesh.shape["lat"], mesh.shape["lon"]

    def local(right_side, depth_level, ocean_mask):
        rows, columns = right_side.shape
        tiles = columns // 128
        ext = rows + 2 * HALO
        deep = rows // 4 + 2 * DEEP

        def level_refs(tiles, total):
            full = pltpu.VMEM((tiles, total + 16, 128), F32)
            return [full] * 8 + [pltpu.VMEM((tiles, total // 2, 128), F32)]

        def exchange_refs(n, width):
            packed = pltpu.VMEM((2, 2, n * width // 128, 128), F32)
            return [packed, packed, pltpu.VMEM((4, 2, 8, 128), F32)]

        return pl.pallas_call(
            functools.partial(kernel, (nlat, nlon)),
            out_shape=[jax.ShapeDtypeStruct((rows, columns), F32)] * 2,
            in_specs=[pl.BlockSpec(memory_space=pl.ANY)] * 3,
            out_specs=[pl.BlockSpec(memory_space=pl.ANY)] * 2,
            scratch_shapes=[
                pltpu.VMEM((2, tiles + 1, ext, 128), F32),
                pltpu.VMEM((tiles, rows, 128), jnp.int32),
                pltpu.VMEM((tiles, rows, 128), jnp.int32),
                pltpu.VMEM((6, 128, 128), BF16),
                pltpu.VMEM((2, 2, deep, 128), F32),
                pltpu.VMEM((ext // 4, 128), F32),
                pltpu.VMEM((2, deep, 128), F32),
                pltpu.VMEM((2, ext // 4, 128), F32),
                *exchange_refs(rows, HALO),
                *exchange_refs(rows // 4, DEEP_LANES),
                pltpu.SemaphoreType.DMA((2, 8)),
                pltpu.SemaphoreType.DMA((2, 8)),
                pltpu.SemaphoreType.DMA((3, tiles)),
                pltpu.SemaphoreType.DMA((2, tiles)),
                *level_refs(tiles + 1, ext),
                *level_refs(3, ext // 2),
                *level_refs(2, deep),
            ],
            compiler_params=pltpu.CompilerParams(collective_id=0, has_side_effects=True),
            name="vcycle",
        )(right_side, depth_level, ocean_mask)

    return jax.shard_map(
        local,
        mesh=mesh,
        in_specs=(P("lat", "lon"),) * 3,
        out_specs=(P("lat", "lon"),) * 2,
        check_vma=False,
    )
```

time: 475 us -> 34.2 us (0.07)
  starting transfers between devices: 173 us -> 0 us
  local copies, waits for them, and re-layouts: 149 us -> 2.72 us
  waiting for transfers between devices: 84.1 us -> 0 us
  other arithmetic: 63.9 us -> 0 us
  Pallas kernels: 0 us -> 30.6 us
    ppermute x88 -> x0, starting transfers between devices: 173 us -> none  [the longest x44 89.1 us: with_halo(): lax.ppermute(tail, axis, [(i, (i + 1) % count) for i in range(ends)])]
    reshape x7 -> x0, local copies, waits for them, and re-layouts: 115 us -> none  [the longest x4 82.3 us: restrict(): return field.reshape(row_count // 2, 2, col_count // 2, 2).mean(axis=(1, 3))]
    ppermute x88 -> x0, waiting for transfers between devices: 84.1 us -> none  [the longest x44 46.5 us: with_halo(): lax.ppermute(tail, axis, [(i, (i + 1) % count) for i in range(ends)])]
    reduce_sum x6 -> x0, other arithmetic: 37.5 us -> none  [restrict(): return field.reshape(row_count // 2, 2, col_count // 2, 2).mean(axis=(1, 3))]
    pallas_call x0 -> x1, Pallas kernels: none -> 30.6 us  [local(): pl.pallas_call(functools.partial(kernel, (nlat, nlon)), out_shape=[jax.Sh...]
    broadcast_in_dim x3 -> x0, local copies, waits for them, and re-layouts: 15.7 us -> none  [prolong(): jnp.broadcast_to(field[:, None, :, None], (row_count, 2, col_count, 2))]
    div x2 -> x0, local copies, waits for them, and re-layouts: 12.6 us -> none  [restrict(): return field.reshape(row_count // 2, 2, col_count // 2, 2).mean(axis=(1, 3))]
    add x17 -> x0, other arithmetic: 9.39 us -> none  [the longest x9 7.14 us: jacobi(): return field + OMEGA * (source - operate(field, coefs, finder)) / coefs[4]]
  transfers between devices with their start and end apart: 88 -> 0, of which waited for: 31 -> 0; matrix products, arithmetic and copies ran while one was open for 32% -> 0% of each run, Pallas kernels for 0% -> 0%
where the time goes in v1:
time: 34.2 us; the launch traced here: 34 us
  Pallas kernels  30.6 us (89%)
  local copies, waits for them, and re-layouts  2.72 us (8%)
  between operations  0.65 us (2%)
    pallas_call x1, Pallas kernels, local(): pl.pallas_call(functools.partial(kernel, (nlat, nlon)), out_shape=[jax.Sh...  30.6 us
    unnamed x4, local copies, waits for them, and re-layouts  2.72 us

profile of v1, /device:TPU:0, one launch (start us, length us, event | category | flops | bytes accessed | tf_op | source)
XLA Modules:
  0.0 34.0 jit_solution(2665359358191397752)
XLA Ops:
  0.6 30.6 %vcycle.1 = (f32[256,512]{1,0:T(8,128)}, f32[256,512]{1,0:T(8,128)}) custom-call(f32[256,512]{1,0:T(8,128)} %right_hbm.1, s32[256,512]{1,0:T(8,128)} %depth_hbm.1, s32[256,512]{1,0:T(8,128)} %mask_hbm.1), custom_call_target="tpu_custom_call" | custom-call | tf_op jit(solution)/shard_map/vcycle/pallas_call | solution.py:438
  31.3 0.0 copy-start
  31.3 1.9 %copy.7 = f32[256,512]{1,0:T(8,128)} copy(f32[256,512]{1,0:T(8,128)} %get-tuple-element.4) | data formatting | bytes 1048576
  33.2 0.0 copy-done
  33.2 0.8 %copy.8 = f32[256,512]{1,0:T(8,128)} copy(f32[256,512]{1,0:T(8,128)S(1)} %copy-done) | data formatting | bytes 1048576
Async XLA Ops:
  31.3 1.9 %copy-start = (f32[256,512]{1,0:T(8,128)S(1)}, f32[256,512]{1,0:T(8,128)}, u32[]{:S(2)}) copy-start(f32[256,512]{1,0:T(8,128)} %get-tuple-element.5) | copy-start | bytes 1572868

commit v2 on v1

--- a/solution.py
+++ b/solution.py
@@ -109,7 +109,7 @@
         self.count, self.unroll = count, unroll
         self.h, self.s, self.ke, self.kn, self.w, self.d, self.a, self.b, self.half = refs
 
-    def coefficients(self):
+    def coefficients(self, source_of=None):
         wrap(self.h, self.count)
 
         def body(j):
@@ -121,10 +121,12 @@
             faces = [a + b + c + d for a, b, c, d in zip(ke, kw, kn, ks)]
             diag = [SIGMA + f for f in faces]
             w = [OMEGA / d for d in diag]
-            s = [jnp.where(f > 0.0, x, 0.0) for f, x in zip(faces, load(self.s, j))]
-            for ref, value in ((self.ke, ke), (self.kn, kn), (self.w, w), (self.d, diag), (self.s, s)):
+            for ref, value in ((self.ke, ke), (self.kn, kn), (self.w, w), (self.d, diag)):
                 store(ref, j, value)
-            store(self.a, j, [x * y for x, y in zip(w, s)])
+            if source_of is not None:
+                s = [jnp.where(f > 0.0, x, 0.0) for f, x in zip(faces, source_of(j))]
+                store(self.s, j, s)
+                store(self.a, j, [x * y for x, y in zip(w, s)])
 
         each(self.count, self.unroll, body)
         wrap(self.kn, self.count)
@@ -157,8 +159,16 @@
 
         each(self.count // 2, self.unroll // 2, body)
 
+    def begin(self, source_of):
+        def body(j):
+            w, d = load(self.w, j), load(self.d, j)
+            s = [jnp.where(x > SIGMA, y, 0.0) for x, y in zip(d, source_of(j))]
+            store(self.s, j, s)
+            store(self.a, j, [x * y for x, y in zip(w, s)])
+
+        each(self.count, self.unroll, body)
+
     def down(self):
-        self.coefficients()
         self.sweep(self.a, self.b)
         wrap(self.b, self.count)
         self.halve(lambda j: self.residual(self.b, j), 0.25)
@@ -176,18 +186,20 @@
 
 
 class Exchange:
-    def __init__(self, x, halo, width, refs, sems):
+    def __init__(self, x, halo, width, refs, sems, fields):
         self.x, self.halo, self.width = x, halo, width
         self.pack, self.got, self.corner = refs
-        self.sems = sems
+        self.sems, self.fields = sems, fields
+        self.part = pl.ds(fields[0], len(fields))
         self.tiles = x.shape[1] - 1
         self.n = x.shape[2] - 2 * halo
         self.groups = 128 // width
 
-    def fill(self, f):
+    def fill(self):
         lane = lanes_of()
+        blocks = range(self.n // 8 // self.groups)
         for side in range(2):
-            for m in range(self.n // 8 // self.groups):
+            for f, m in ((f, m) for f in self.fields for m in blocks):
                 total = None
                 for g in range(self.groups):
                     row = self.halo + 8 * (m * self.groups + g)
@@ -214,15 +226,15 @@
             copy.start()
             copies.append(copy)
 
-        h, n, last = self.halo, self.n, self.pack.shape[2] - 8
+        h, n, last, p = self.halo, self.n, self.pack.shape[2] - 8, self.part
         for side, dlon in ((0, -1), (1, 1)):
-            send(self.pack.at[side], self.got.at[side], 0, dlon)
+            send(self.pack.at[side, p], self.got.at[side, p], 0, dlon)
         for side, dlon in ((0, -1), (1, 1)):
-            send(self.pack.at[side, :, pl.ds(last, 8), :], self.corner.at[side], 1, dlon)
-            send(self.pack.at[side, :, pl.ds(0, 8), :], self.corner.at[2 + side], -1, dlon)
+            send(self.pack.at[side, p, pl.ds(last, 8), :], self.corner.at[side, p], 1, dlon)
+            send(self.pack.at[side, p, pl.ds(0, 8), :], self.corner.at[2 + side, p], -1, dlon)
         core = pl.ds(0, self.tiles)
-        send(self.x.at[:, core, pl.ds(n, h), :], self.x.at[:, core, pl.ds(0, h), :], 1, 0)
-        send(self.x.at[:, core, pl.ds(h, h), :], self.x.at[:, core, pl.ds(h + n, h), :], -1, 0)
+        send(self.x.at[p, core, pl.ds(n, h), :], self.x.at[p, core, pl.ds(0, h), :], 1, 0)
+        send(self.x.at[p, core, pl.ds(h, h), :], self.x.at[p, core, pl.ds(h + n, h), :], -1, 0)
         self.copies = copies
 
     def finish(self, place):
@@ -232,7 +244,7 @@
         lane = lanes_of()
         edge, total = self.halo // 8, self.x.shape[2] // 8
         count = self.n // 8
-        for f in range(2):
+        for f in self.fields:
             for b in range(total):
                 a = b - edge
                 if a < 0:
@@ -254,15 +266,15 @@
                 self.x[f, self.tiles, 8 * b : 8 * b + 8, :] = tile
         for blocks, pole in ((range(edge), lat == 0), (range(total - edge, total), lat == nlat - 1)):
             keep = jnp.where(pole, 0.0, 1.0)
-            for f in range(2):
+            for f in self.fields:
                 for t in range(self.tiles + 1):
                     for b in blocks:
                         self.x[f, t, 8 * b : 8 * b + 8, :] = self.x[f, t, 8 * b : 8 * b + 8, :] * keep
 
 
-def kernel(place_of, right_hbm, depth_hbm, mask_hbm, press_hbm, resid_hbm, x0, depth, mask, mats, x2, y2, z2, c1, *rest):
+def kernel(place_of, right_hbm, depth_hbm, mask_hbm, out, x0, depth, mask, mats, x2, y2, z2, c1, hp, hq, *rest):
     nlat, nlon = place_of
-    pack0, got0, corner0, pack2, got2, corner2, sems0, sems2, in_sems, out_sems = rest[:10]
+    pack0, got0, corner0, pack2, got2, corner2, sems0, sems2, in_sems, sems1 = rest[:10]
     refs0, refs1, refs2 = rest[10:19], rest[19:28], rest[28:37]
     lat, lon = lax.axis_index("lat"), lax.axis_index("lon")
     place = (lat, lon, nlat, nlon)
@@ -305,65 +317,70 @@
         copy.wait()
     for t in range(tiles):
         x0[0, t, HALO : HALO + rows, :] = (depth[t] * mask[t]).astype(F32)
-    outer = Exchange(x0, HALO, HALO, (pack0, got0, corner0), sems0)
-    outer.fill(0)
-    outer.fill(1)
+    outer = Exchange(x0, HALO, HALO, (pack0, got0, corner0), sems0, (0, 1))
+    outer.fill()
     pl.semaphore_wait(barrier, 8)
     outer.start(place)
+
+    for t in range(tiles):
+        for a in range(rows // 16):
+            pair = [x0[0, t, pl.ds(HALO + 16 * a + i, 8, stride=2), :] for i in range(2)]
+            hp[t, 8 * a : 8 * a + 8, :] = pair[0] + pair[1]
+    for t, x in enumerate(shrink([hp[t] for t in range(tiles)], mats, 1)):
+        hq[t] = x
+    for t in range(tiles // 2):
+        for a in range(rows // 32):
+            pair = [hq[t, pl.ds(16 * a + i, 8, stride=2), :] for i in range(2)]
+            hp[t, 8 * a : 8 * a + 8, :] = pair[0] + pair[1]
+    deep_rows = rows // 4
+    x2[0, 0, DEEP : DEEP + deep_rows, :] = shrink([hp[t, 0:deep_rows, :] for t in range(2)], mats, 2)[0]
+    deep_height = Exchange(x2, DEEP, DEEP_LANES, (pack2, got2, corner2), sems1, (0,))
+    deep_height.fill()
+    deep_height.start(place)
     outer.finish(place)
 
     count0 = refs0[0].shape[1] // 8 - 2
     count1 = refs1[0].shape[1] // 8 - 2
     count2 = refs2[0].shape[1] // 8 - 2
-    level0 = Level(0, count0, 4, refs0)
-    level1 = Level(1, count1, 6, refs1)
+    level0 = Level(0, count0, 12, refs0)
+    level1 = Level(1, count1, 18, refs1)
     level2 = Level(2, count2, count2, refs2)
     for j in range(count0):
         for t in range(tiles + 1):
             level0.h[t, at(j), :] = x0[0, t, pl.ds(j, 8, stride=count0), :]
-            level0.s[t, at(j), :] = x0[1, t, pl.ds(j, 8, stride=count0), :]
 
     level0.halve(lambda j: load(level0.h, j), 1.0)
     for t, x in enumerate(shrink([level0.half[t] for t in range(tiles + 1)], mats, 1)):
         level1.h[t, 8 : 8 + 8 * count1, :] = x
+    level0.coefficients(lambda j: [x0[1, t, pl.ds(j, 8, stride=count0), :] for t in range(tiles + 1)])
     level0.down()
     for t, x in enumerate(shrink([level0.half[t] for t in range(tiles + 1)], mats, 3)):
         level1.s[t, 8 : 8 + 8 * count1, :] = x
 
     half1 = count1 // 2
     margin = HALO // 4
-    deep_rows = x2.shape[2] - 2 * DEEP
-
-    def pass_down(f, parts):
-        out = shrink([level1.half[0], level1.half[1]], mats, parts)[0]
-        for j in range(half1):
-            y2[pl.ds(j, 8, stride=half1), :] = out[8 * j : 8 * j + 8]
-        for a in range(deep_rows // 8):
-            x2[f, 0, DEEP + 8 * a : DEEP + 8 * a + 8, :] = y2[margin + 8 * a : margin + 8 * a + 8, :]
-
-    level1.halve(lambda j: load(level1.h, j), 1.0)
-    pass_down(0, 2)
+    level1.coefficients(lambda j: load(level1.s, j))
     level1.down()
-    pass_down(1, 3)
-
-    inner = Exchange(x2, DEEP, DEEP_LANES, (pack2, got2, corner2), sems2)
-    inner.fill(0)
-    inner.fill(1)
+    fallen = shrink([level1.half[0], level1.half[1]], mats, 3)[0]
+    for j in range(half1):
+        y2[pl.ds(j, 8, stride=half1), :] = fallen[8 * j : 8 * j + 8]
+    for a in range(deep_rows // 8):
+        x2[1, 0, DEEP + 8 * a : DEEP + 8 * a + 8, :] = y2[margin + 8 * a : margin + 8 * a + 8, :]
+
+    inner = Exchange(x2, DEEP, DEEP_LANES, (pack2, got2, corner2), sems2, (1,))
+    inner.fill()
     inner.start(place)
-    inner.finish(place)
+    deep_height.finish(place)
     for j in range(count2):
         for t in range(2):
             level2.h[t, at(j), :] = x2[0, t, pl.ds(j, 8, stride=count2), :]
-            level2.s[t, at(j), :] = x2[1, t, pl.ds(j, 8, stride=count2), :]
     count3 = count2 // 2
+    level2.coefficients()
     level2.halve(lambda j: load(level2.h, j), 1.0)
     height = shrink([level2.half[0], level2.half[1]], mats, 2)[0]
-    level2.down()
-    source = shrink([level2.half[0], level2.half[1]], mats, 3)[0]
 
     scale = 0.0625**3 / DEPTH_LEVELS
     h = [height[8 * j : 8 * j + 8] for j in range(count3)]
-    s = [source[8 * j : 8 * j + 8] for j in range(count3)]
 
     def north(v):
         return v[1:] + [upper(v[0])]
@@ -373,7 +390,12 @@
     ks = [lower(kn[-1])] + kn[:-1]
     faces = [a + pltpu.roll(a, 1, 1) + b + c for a, b, c in zip(ke, kn, ks)]
     w = [OMEGA / (SIGMA + f) for f in faces]
-    s = [jnp.where(f > 0.0, x, 0.0) for f, x in zip(faces, s)]
+
+    inner.finish(place)
+    level2.begin(lambda j: [x2[1, t, pl.ds(j, 8, stride=count2), :] for t in range(2)])
+    level2.down()
+    source = shrink([level2.half[0], level2.half[1]], mats, 3)[0]
+    s = [jnp.where(f > 0.0, source[8 * j : 8 * j + 8], 0.0) for j, f in enumerate(faces)]
     v = [x * y for x, y in zip(w, s)]
     for _ in range(COARSE_SWEEPS - 1):
         up, down = north(v), [lower(v[-1])] + v[:-1]
@@ -401,18 +423,23 @@
         level0.half[t] = x
     level0.up()
     wrap(level0.b, count0)
-    each(count0, 4, lambda j: store(level0.a, j, level0.residual(level0.b, j)))
-
+
+    def last(j):
+        pressure, residual = load(level0.b, j), level0.residual(level0.b, j)
+        for t in range(tiles):
+            out[0, t, pl.ds(j, 8, stride=count0), :] = pressure[t]
+            out[1, t, pl.ds(j, 8, stride=count0), :] = residual[t]
+
+    each(count0, level0.unroll, last)
+
+
+def hand_out(out, press_hbm, resid_hbm, sems):
+    rows = press_hbm.shape[0]
     stores = []
-    for i, (ref, out) in enumerate(((level0.b, press_hbm), (level0.a, resid_hbm))):
-        for t in range(tiles):
-            for j in range(count0):
-                x0[i, t, pl.ds(j, 8, stride=count0), :] = ref[t, at(j), :]
-            stores.append(
-                pltpu.make_async_copy(
-                    x0.at[i, t, pl.ds(HALO, rows), :], out.at[:, pl.ds(128 * t, 128)], out_sems.at[i, t]
-                )
-            )
+    for i, ref in enumerate((press_hbm, resid_hbm)):
+        for t in range(out.shape[1]):
+            src = out.at[i, t, pl.ds((out.shape[2] - rows) // 2, rows), :]
+            stores.append(pltpu.make_async_copy(src, ref.at[:, pl.ds(128 * t, 128)], sems.at[i, t]))
             stores[-1].start()
     for copy in stores:
         copy.wait()
@@ -435,11 +462,11 @@
             packed = pltpu.VMEM((2, 2, n * width // 128, 128), F32)
             return [packed, packed, pltpu.VMEM((4, 2, 8, 128), F32)]
 
-        return pl.pallas_call(
+        both = pl.pallas_call(
             functools.partial(kernel, (nlat, nlon)),
-            out_shape=[jax.ShapeDtypeStruct((rows, columns), F32)] * 2,
+            out_shape=pltpu.VMEM((2, tiles, ext, 128), F32),
             in_specs=[pl.BlockSpec(memory_space=pl.ANY)] * 3,
-            out_specs=[pl.BlockSpec(memory_space=pl.ANY)] * 2,
+            out_specs=pl.BlockSpec(memory_space=pltpu.VMEM),
             scratch_shapes=[
                 pltpu.VMEM((2, tiles + 1, ext, 128), F32),
                 pltpu.VMEM((tiles, rows, 128), jnp.int32),
@@ -449,19 +476,30 @@
                 pltpu.VMEM((ext // 4, 128), F32),
                 pltpu.VMEM((2, deep, 128), F32),
                 pltpu.VMEM((2, ext // 4, 128), F32),
+                pltpu.VMEM((tiles, rows // 2, 128), F32),
+                pltpu.VMEM((tiles // 2, rows // 2, 128), F32),
                 *exchange_refs(rows, HALO),
                 *exchange_refs(rows // 4, DEEP_LANES),
                 pltpu.SemaphoreType.DMA((2, 8)),
                 pltpu.SemaphoreType.DMA((2, 8)),
                 pltpu.SemaphoreType.DMA((3, tiles)),
-                pltpu.SemaphoreType.DMA((2, tiles)),
+                pltpu.SemaphoreType.DMA((2, 8)),
                 *level_refs(tiles + 1, ext),
                 *level_refs(3, ext // 2),
                 *level_refs(2, deep),
             ],
-            compiler_params=pltpu.CompilerParams(collective_id=0, has_side_effects=True),
+            compiler_params=pltpu.CompilerParams(collective_id=0, has_side_effects=True, vmem_limit_bytes=67_043_328 - (2 * tiles * ext + 256) * 512),
             name="vcycle",
         )(right_side, depth_level, ocean_mask)
+        return pl.pallas_call(
+            hand_out,
+            out_shape=[jax.ShapeDtypeStruct((rows, columns), F32)] * 2,
+            in_specs=[pl.BlockSpec(memory_space=pltpu.VMEM)],
+            out_specs=[pl.BlockSpec(memory_space=pl.ANY)] * 2,
+            scratch_shapes=[pltpu.SemaphoreType.DMA((2, tiles))],
+            compiler_params=pltpu.CompilerParams(vmem_limit_bytes=8 * 2**20),
+            name="hand_out",
+        )(both)
 
     return jax.shard_map(
         local,

time: 34.2 us -> 26.4 us (0.77)
  Pallas kernels: 30.6 us -> 25.6 us
  local copies, waits for them, and re-layouts: 2.72 us -> 0 us
    pallas_call x1 -> x2, Pallas kernels: 30.6 us -> 25.6 us  [the longest x1 24.6 us: local(): pl.pallas_call(functools.partial(kernel, (nlat, nlon)), out_shape=pltpu.V...]
    unnamed x4 -> x0, local copies, waits for them, and re-layouts: 2.72 us -> none
where the time goes in v2:
time: 26.4 us; the launch traced here: 26.2 us
  Pallas kernels  25.6 us (97%)
  between operations  0.64 us (2%)
    pallas_call x1, Pallas kernels, local(): pl.pallas_call(functools.partial(kernel, (nlat, nlon)), out_shape=pltpu.V...  24.6 us
    pallas_call x1, Pallas kernels, local(): pl.pallas_call(hand_out, out_shape=[jax.ShapeDtypeStruct((rows, columns),...  1.03 us

profile of v2, /device:TPU:0, one launch (start us, length us, event | category | flops | bytes accessed | tf_op | source)
XLA Modules:
  0.0 26.2 jit_solution(5512955678876940226)
XLA Ops:
  0.6 24.6 %vcycle.1.out = f32[2,4,288,128]{3,2,1,0:T(8,128)S(1)} custom-call(f32[256,512]{1,0:T(8,128)} %right_hbm.1, s32[256,512]{1,0:T(8,128)} %depth_hbm.1, s32[256,512]{1,0:T(8,128)} %mask_hbm.1), custom_call_target="tpu_custom_call" | custom-call | tf_op jit(solution)/shard_map/vcycle/pallas_call | solution.py:465
  25.2 1.0 %hand_out.1 = (f32[256,512]{1,0:T(8,128)}, f32[256,512]{1,0:T(8,128)}) custom-call(f32[2,4,288,128]{3,2,1,0:T(8,128)S(1)} %vcycle.1.out), custom_call_target="tpu_custom_call" | custom-call | tf_op jit(solution)/shard_map/hand_out/pallas_call | solution.py:494
